TPU v7x, 128 devices: a whole 4x4x4 slice. The times are simulated.
128 devices in a mesh: fsdp: 16 (over z_lo, y, core), tp: 8 (over x, z_hi).
Axes of the slice: x: 4, y: 4, z: 4 (z_hi: 2, z_lo: 2; z = z_hi * 2 + z_lo), core: 2. Of those that a mesh axis runs over, the one named last changes fastest.
Arguments:
- probe_states: bfloat16 [256, 16384], P('fsdp'), may hold values from -6 to 6
- wq_master: float32 [16384, 4096], P(('fsdp', 'tp')), may hold values from -1 to 1
- wq_first: float32 [16384, 4096], P(('fsdp', 'tp')), may hold values from -6 to 6
- wq_second: float32 [16384, 4096], P(('fsdp', 'tp')), may hold values from 0.25 to 4
- wq_grad: float32 [16384, 4096], P('fsdp', 'tp'), may hold values from -6 to 6
- wkv_master: float32 [16384, 512], P(('fsdp', 'tp')), may hold values from -0.046875 to 0.046875
- wkv_first: float32 [16384, 512], P(('fsdp', 'tp')), may hold values from -6 to 6
- wkv_second: float32 [16384, 512], P(('fsdp', 'tp')), may hold values from 0.25 to 4
- wkv_grad: float32 [16384, 512], P(('fsdp', 'tp')), may hold values from -6 to 6
Outputs:
- wq_updated: float32 [16384, 4096], P('fsdp', 'tp')
- wq_first_new: float32 [16384, 4096], P('fsdp', 'tp')
- wq_second_new: float32 [16384, 4096], P('fsdp', 'tp')
- wkv_updated: float32 [16384, 512], P(('fsdp', 'tp'))
- wkv_first_new: float32 [16384, 512], P(('fsdp', 'tp'))
- wkv_second_new: float32 [16384, 512], P(('fsdp', 'tp'))
- probe_query: bfloat16 [256, 4096], P('fsdp', 'tp')
- probe_keyvalue: bfloat16 [256, 512], replicated
All inputs are finite; a program needn't handle non-finite values.
Results may differ from a plain program's by a relative error of at most 0.008.
Values may be sent and summed in bfloat16 or wider, within the bound.
A program may use at most 128 MiB of HBM per device.

v0:
```python
import math
import jax
import jax.numpy as jnp
from jax import lax
from jax.sharding import PartitionSpec as P

BETA_ONE = 0.9
BETA_TWO = 0.95
LEARN_RATE = 0.001
EPSILON = 1e-08
CORRECT_ONE = 1.0 - math.exp(1000.0 * math.log(0.9))
CORRECT_TWO = 1.0 - math.exp(1000.0 * math.log(0.95))


def adam_step(master, first, second, grad):
    first_new = BETA_ONE * first + (1.0 - BETA_ONE) * grad
    second_new = BETA_TWO * second + (1.0 - BETA_TWO) * grad * grad
    update = first_new / CORRECT_ONE / (jnp.sqrt(second_new / CORRECT_TWO) + EPSILON)
    return (master - LEARN_RATE * update, first_new, second_new)


def body(
    probe_states,
    wq_master,
    wq_first,
    wq_second,
    wq_grad,
    wkv_master,
    wkv_first,
    wkv_second,
    wkv_grad,
):
    master, first, second = (
        lax.all_to_all(wq_master, "tp", split_axis=1, concat_axis=0, tiled=True),
        lax.all_to_all(wq_first, "tp", split_axis=1, concat_axis=0, tiled=True),
        lax.all_to_all(wq_second, "tp", split_axis=1, concat_axis=0, tiled=True),
    )
    wq_new, wq_mom, wq_var = adam_step(master, first, second, wq_grad)
    wkv_new, wkv_mom, wkv_var = adam_step(wkv_master, wkv_first, wkv_second, wkv_grad)
    columns = lax.all_to_all(probe_states, "fsdp", split_axis=1, concat_axis=0, tiled=True)
    tp_rank = lax.axis_index("tp")
    kv_rows = wkv_master.shape[0]
    own_columns = lax.dynamic_slice_in_dim(columns, tp_rank * kv_rows, kv_rows, 1)
    kv_term = jnp.dot(own_columns, wkv_new.astype(jnp.bfloat16), preferred_element_type=jnp.float32)
    probe_keyvalue = lax.psum(kv_term, ("fsdp", "tp")).astype(jnp.bfloat16)
    wq_low = wq_new.astype(jnp.bfloat16)
    queries = jnp.dot(
        probe_states,
        lax.all_gather(wq_low, "fsdp", axis=0, tiled=True),
        preferred_element_type=jnp.float32,
    )
    probe_query = queries.astype(jnp.bfloat16)
    return (wq_new, wq_mom, wq_var, wkv_new, wkv_mom, wkv_var, probe_query, probe_keyvalue)


def solution(mesh):
    return jax.shard_map(
        body,
        mesh=mesh,
        in_specs=(
            P("fsdp", None),
            P(("fsdp", "tp"), None),
            P(("fsdp", "tp"), None),
            P(("fsdp", "tp"), None),
            P("fsdp", "tp"),
            P(("fsdp", "tp"), None),
            P(("fsdp", "tp"), None),
            P(("fsdp", "tp"), None),
            P(("fsdp", "tp"), None),
        ),
        out_specs=(
            P("fsdp", "tp"),
            P("fsdp", "tp"),
            P("fsdp", "tp"),
            P(("fsdp", "tp"), None),
            P(("fsdp", "tp"), None),
            P(("fsdp", "tp"), None),
            P("fsdp", "tp"),
            P(),
        ),
        check_vma=False,
    )
```

profile of v0, /device:TPU:1, one launch (start us, length us, event | category | flops | bytes accessed | tf_op | source)
XLA Modules:
  0.0 238.8 jit_solution(16143131540047762686)
XLA Ops:
  7.2 3.1 %copy.39 = f32[16,8,8,512]{3,2,0,1:T(8,128)} copy(f32[16,8,8,512]{3,2,1,0:T(8,128)} %bitcast.42) | data formatting | bytes 4194304 | tf_op jit(solution)/shard_map/all_to_all | solution.py:36
  10.3 8.2 %all-to-all-start.2 = ((f32[128,8,512]{2,0,1:T(8,128)}), f32[128,8,512]{2,0,1:T(8,128)S(1)}, u32[]{:S(2)}, u32[]{:S(2)}) async-start(f32[128,8,512]{2,0,1:T(8,128)} %bitcast.40), calls=%async_computation.2 | async-start | bytes 4194304 | tf_op jit(solution)/shard_map/all_to_all | solution.py:36
  18.5 3.1 %copy.40 = f32[16,8,8,512]{3,2,0,1:T(8,128)} copy(f32[16,8,8,512]{3,2,1,0:T(8,128)} %bitcast.43) | data formatting | bytes 4194304 | tf_op jit(solution)/shard_map/all_to_all | solution.py:35
  21.6 27.5 %all-to-all-done.2 = f32[128,8,512]{2,0,1:T(8,128)S(1)} async-done(((f32[128,8,512]{2,0,1:T(8,128)}), f32[128,8,512]{2,0,1:T(8,128)S(1)}, u32[]{:S(2)}, u32[]{:S(2)}) %all-to-all-start.2) | async-done | bytes 2097184 | tf_op jit(solution)/shard_map/all_to_all | solution.py:36
  49.1 0.0 copy-start
  49.1 1.3 copy-done
  50.4 4.4 %all-to-all-start.1 = ((f32[128,8,512]{2,0,1:T(8,128)}), f32[128,8,512]{2,0,1:T(8,128)}, u32[]{:S(2)}, u32[]{:S(2)}) async-start(f32[128,8,512]{2,0,1:T(8,128)} %bitcast.39), calls=%async_computation.1 | async-start | bytes 4194304 | tf_op jit(solution)/shard_map/all_to_all | solution.py:35
  54.8 3.2 %copy.41 = f32[16,8,8,512]{3,2,0,1:T(8,128)} copy(f32[16,8,8,512]{3,2,1,0:T(8,128)} %bitcast.44) | data formatting | bytes 4194304 | tf_op jit(solution)/shard_map/all_to_all | solution.py:34
  57.9 26.7 %all-to-all-done.1 = f32[128,8,512]{2,0,1:T(8,128)} async-done(((f32[128,8,512]{2,0,1:T(8,128)}), f32[128,8,512]{2,0,1:T(8,128)}, u32[]{:S(2)}, u32[]{:S(2)}) %all-to-all-start.1) | async-done | bytes 2097184 | tf_op jit(solution)/shard_map/all_to_all | solution.py:35
  84.6 3.6 %all-to-all-start = ((f32[128,8,512]{2,0,1:T(8,128)}), f32[128,8,512]{2,0,1:T(8,128)S(1)}, u32[]{:S(2)}, u32[]{:S(2)}) async-start(f32[128,8,512]{2,0,1:T(8,128)} %bitcast.38), calls=%async_computation | async-start | bytes 4194304 | tf_op jit(solution)/shard_map/all_to_all | solution.py:34
  88.2 0.0 all-gather.2.cloned.1.call-start
  88.2 3.3 %broadcast_multiply_fusion = f32[128,8,512]{2,0,1:T(8,128)} fusion(f32[128,8,512]{2,0,1:T(8,128)} %copy-done), kind=kLoop, calls=%fused_computation.9 | loop fusion | flops 524288 | bytes 4194304 | tf_op jit(solution)/shard_map/mul | solution.py:17
  91.5 3.3 %broadcast_multiply_fusion.1 = f32[128,8,512]{2,0,1:T(8,128)} fusion(f32[128,8,512]{2,0,1:T(8,128)} %all-to-all-done.1), kind=kLoop, calls=%fused_computation.10 | loop fusion | flops 524288 | bytes 4194304 | tf_op jit(solution)/shard_map/mul | solution.py:16
  94.8 0.0 copy-start.1
  94.8 22.8 %all-to-all-done = f32[128,8,512]{2,0,1:T(8,128)S(1)} async-done(((f32[128,8,512]{2,0,1:T(8,128)}), f32[128,8,512]{2,0,1:T(8,128)S(1)}, u32[]{:S(2)}, u32[]{:S(2)}) %all-to-all-start) | async-done | bytes 2097184 | tf_op jit(solution)/shard_map/all_to_all | solution.py:34
  117.5 6.7 %fusion.7 = (bf16[1024,512]{1,0:T(8,128)(2,1)}, f32[1024,512]{1,0:T(8,128)}, f32[1024,512]{1,0:T(8,128)}, f32[1024,512]{1,0:T(8,128)}) fusion(f32[128,8,512]{2,0,1:T(8,128)S(1)} %all-to-all-done, f32[1024,512]{1,0:T(8,128)} %param.13, f32[128,8,512]{2,0,1:T(8,128)} %broadcast_multiply_fusion, f32[128,8,512]{2,0,1:T(8,128)} %broadcast_multiply_fusion.1), kind=kLoop, calls=%fused_computation.20 | loop fusion | flops 5242880 | bytes 15728640 | tf_op jit(solution)/shard_map/convert_element_type | solution.py:46
  124.3 0.0 copy-start.6
  124.3 0.0 all-gather.2.cloned.1.call-update
  124.3 0.0 copy-done.1
  124.3 0.9 copy.42
  125.2 7.0 %all-to-all-start.3 = ((bf16[16,16,1024]{2,0,1:T(8,128)(2,1)}), bf16[16,16,1024]{2,0,1:T(8,128)(2,1)S(1)}, u32[]{:S(2)}, u32[]{:S(2)}) async-start(bf16[16,16,1024]{2,0,1:T(8,128)(2,1)} %bitcast.37), calls=%async_computation.3 | async-start | bytes 1048576 | tf_op jit(solution)/shard_map/all_to_all | solution.py:40
  132.2 0.0 copy-done.3
  132.2 0.0 copy-done.4
  132.2 0.0 copy-done.5
  132.2 0.0 copy-done.6
  132.2 0.9 multiply_subtract_fusion
  133.2 13.5 %all-to-all-done.3 = bf16[16,16,1024]{2,0,1:T(8,128)(2,1)S(1)} async-done(((bf16[16,16,1024]{2,0,1:T(8,128)(2,1)}), bf16[16,16,1024]{2,0,1:T(8,128)(2,1)S(1)}, u32[]{:S(2)}, u32[]{:S(2)}) %all-to-all-start.3) | async-done | bytes 524320 | tf_op jit(solution)/shard_map/all_to_all | solution.py:40
  146.6 0.2 fusion.3
  146.8 68.1 %all-reduce.1 = bf16[256,512]{1,0:T(8,128)(2,1)} all-reduce(f32[256,512]{1,0:T(8,128)S(1)} %fusion.3), channel_id=1, replica_groups=mesh['fsdp'=16,'tp'=8] {'fsdp','tp'}, use_global_device_ids=true, to_apply=%region_0.0 | all-reduce | flops 131072 | bytes 786432 | tf_op jit(solution)/shard_map/psum | solution.py:45
  214.9 8.3 %all-gather.2.cloned.1.call-done = bf16[16384,512]{1,0:T(8,128)(2,1)} async-done(((bf16[1024,512]{1,0:T(8,128)(2,1)}), bf16[16384,512]{1,0:T(8,128)(2,1)}) %all-gather.2.cloned.1.call-update) | async-done | bytes 16777232 | tf_op jit(solution)/shard_map/all_gather | solution.py:49
  223.3 8.6 %fusion.1 = bf16[16,512]{1,0:T(8,128)(2,1)} fusion(bf16[16,16384]{1,0:T(8,128)(2,1)S(1)} %copy-done.1, bf16[16384,512]{1,0:T(8,128)(2,1)} %all-gather.2.cloned.1.call-done), kind=kOutput, calls=%fused_computation.8 | convolution fusion | flops 268443648 | bytes 17317888 | tf_op jit(solution)/shard_map/dot_general | solution.py:47
  231.9 0.0 copy-done.2
  (4 shorter events, 0.0 us)
Async XLA Ops:
  10.3 38.8 %all-to-all-start.2 = ((f32[128,8,512]{2,0,1:T(8,128)}), f32[128,8,512]{2,0,1:T(8,128)S(1)}, u32[]{:S(2)}, u32[]{:S(2)}) async-start(f32[128,8,512]{2,0,1:T(8,128)} %bitcast.40), calls=%async_computation.2 | async-start | bytes 4194304 | tf_op jit(solution)/shard_map/all_to_all | solution.py:36
  49.1 1.3 copy-start
  50.4 34.2 %all-to-all-start.1 = ((f32[128,8,512]{2,0,1:T(8,128)}), f32[128,8,512]{2,0,1:T(8,128)}, u32[]{:S(2)}, u32[]{:S(2)}) async-start(f32[128,8,512]{2,0,1:T(8,128)} %bitcast.39), calls=%async_computation.1 | async-start | bytes 4194304 | tf_op jit(solution)/shard_map/all_to_all | solution.py:35
  84.6 33.0 %all-to-all-start = ((f32[128,8,512]{2,0,1:T(8,128)}), f32[128,8,512]{2,0,1:T(8,128)S(1)}, u32[]{:S(2)}, u32[]{:S(2)}) async-start(f32[128,8,512]{2,0,1:T(8,128)} %bitcast.38), calls=%async_computation | async-start | bytes 4194304 | tf_op jit(solution)/shard_map/all_to_all | solution.py:34
  88.2 135.1 %all-gather.2.cloned.1.call-start = ((), (), s32[]{:S(2)}) async-start(), calls=%async_computation.4 | async-start | bytes 17825792 | tf_op jit(solution)/shard_map/all_gather | solution.py:49
  94.8 29.5 %copy-start.1 = (bf16[16,16384]{1,0:T(8,128)(2,1)S(1)}, bf16[16,16384]{1,0:T(8,128)(2,1)}, u32[]{:S(2)}) copy-start(bf16[16,16384]{1,0:T(8,128)(2,1)} %param.9) | copy-start | bytes 1572868
  124.3 7.9 %copy-start.3 = (f32[128,512]{1,0:T(8,128)S(1)}, f32[128,512]{1,0:T(8,128)}, u32[]{:S(2)}) copy-start(f32[128,512]{1,0:T(8,128)} %param.14) | copy-start | bytes 786436
  124.3 7.9 %copy-start.4 = (f32[128,512]{1,0:T(8,128)S(1)}, f32[128,512]{1,0:T(8,128)}, u32[]{:S(2)}) copy-start(f32[128,512]{1,0:T(8,128)} %param.17) | copy-start | bytes 786436
  124.3 7.9 %copy-start.5 = (f32[128,512]{1,0:T(8,128)S(1)}, f32[128,512]{1,0:T(8,128)}, u32[]{:S(2)}) copy-start(f32[128,512]{1,0:T(8,128)} %param.16) | copy-start | bytes 786436
  124.3 7.9 %copy-start.6 = (f32[128,512]{1,0:T(8,128)S(1)}, f32[128,512]{1,0:T(8,128)}, u32[]{:S(2)}) copy-start(f32[128,512]{1,0:T(8,128)} %param.15) | copy-start | bytes 786436
  125.2 21.4 %all-to-all-start.3 = ((bf16[16,16,1024]{2,0,1:T(8,128)(2,1)}), bf16[16,16,1024]{2,0,1:T(8,128)(2,1)S(1)}, u32[]{:S(2)}, u32[]{:S(2)}) async-start(bf16[16,16,1024]{2,0,1:T(8,128)(2,1)} %bitcast.37), calls=%async_computation.3 | async-start | bytes 1048576 | tf_op jit(solution)/shard_map/all_to_all | solution.py:40
  133.1 98.8 %copy-start.2 = (f32[128,512]{1,0:T(8,128)}, f32[128,512]{1,0:T(8,128)S(1)}, u32[]{:S(2)}) copy-start(f32[128,512]{1,0:T(8,128)S(1)} %get-tuple-element.12) | copy-start | bytes 786436
Sparse Core Ops, SparseCore 0:
  124.5 98.7 all-gather.1
where the time goes:
time: 239 us
  waiting for transfers between devices  98.7 us (41%)
  blocking collectives  68.1 us (28%)
  starting transfers between devices  23.1 us (10%)
  other arithmetic  14.3 us (6%)
  between operations  14.1 us (6%)
  local copies, waits for them, and re-layouts  11.7 us (5%)
  matrix products  8.86 us (4%)
    psum x1, blocking collectives, body(): probe_keyvalue = lax.psum(kv_term, ('fsdp', 'tp')).astype(jnp.bfloat16)  68.1 us
    all_to_all x1, waiting for transfers between devices, body(): lax.all_to_all(wq_second, 'tp', split_axis=1, concat_axis=0, tiled=True)  27.5 us
    all_to_all x1, waiting for transfers between devices, body(): lax.all_to_all(wq_first, 'tp', split_axis=1, concat_axis=0, tiled=True)  26.7 us
    all_to_all x1, waiting for transfers between devices, body(): lax.all_to_all(wq_master, 'tp', split_axis=1, concat_axis=0, tiled=True)  22.8 us
    all_to_all x1, waiting for transfers between devices, body(): lax.all_to_all(probe_states, 'fsdp', split_axis=1, concat_axis=0, tiled=T...  13.5 us
    dot_general x1, matrix products, body(): jnp.dot(probe_states, lax.all_gather(wq_low, 'fsdp', axis=0, tiled=True),...  8.65 us
    all_gather x1, waiting for transfers between devices, body(): lax.all_gather(wq_low, 'fsdp', axis=0, tiled=True)  8.34 us
    all_to_all x1, starting transfers between devices, body(): lax.all_to_all(wq_second, 'tp', split_axis=1, concat_axis=0, tiled=True)  8.15 us
  transfers between devices with their start and end apart: 5, of which 5 were waited for; matrix products, arithmetic and copies ran while one was open for 6% of the time, Pallas kernels for 0%

commit v1 on v0

--- a/solution.py
+++ b/solution.py
@@ -42,7 +42,7 @@
     kv_rows = wkv_master.shape[0]
     own_columns = lax.dynamic_slice_in_dim(columns, tp_rank * kv_rows, kv_rows, 1)
     kv_term = jnp.dot(own_columns, wkv_new.astype(jnp.bfloat16), preferred_element_type=jnp.float32)
-    probe_keyvalue = lax.psum(kv_term, ("fsdp", "tp")).astype(jnp.bfloat16)
+    probe_keyvalue = jnp.sum(lax.all_gather(kv_term, ("fsdp", "tp")), axis=0).astype(jnp.bfloat16)
     wq_low = wq_new.astype(jnp.bfloat16)
     queries = jnp.dot(
         probe_states,

time: 239 us -> 632 us (2.64)
  waiting for transfers between devices: 98.7 us -> 537 us
  blocking collectives: 68.1 us -> 0 us
  other arithmetic: 14.3 us -> 35.8 us
    all_gather x0 -> x1, waiting for transfers between devices: none -> 374 us  [body(): lax.all_gather(kv_term, ('fsdp', 'tp'))]
    psum x1 -> x0, blocking collectives: 68.1 us -> none  [body(): probe_keyvalue = lax.psum(kv_term, ('fsdp', 'tp')).astype(jnp.bfloat16)]
    all_gather x1, waiting for transfers between devices: 8.34 us -> 72.7 us  [body(): lax.all_gather(wq_low, 'fsdp', axis=0, tiled=True)]
    reduce_sum x0 -> x1, other arithmetic: none -> 21.6 us  [body(): jnp.sum(lax.all_gather(kv_term, ('fsdp', 'tp')), axis=0)]
  transfers between devices with their start and end apart: 5 -> 6, of which waited for: 5 -> 6; matrix products, arithmetic and copies ran while one was open for 6% -> 4% of each run, Pallas kernels for 0% -> 0%
where the time goes in v1:
time: 632 us; the launch traced here: 631 us
  waiting for transfers between devices  537 us (85%)
  other arithmetic  35.8 us (6%)
  starting transfers between devices  23.2 us (4%)
  between operations  14.1 us (2%)
  local copies, waits for them, and re-layouts  11.6 us (2%)
  matrix products  9.68 us (2%)
    all_gather x1, waiting for transfers between devices, body(): lax.all_gather(kv_term, ('fsdp', 'tp'))  374 us
    all_gather x1, waiting for transfers between devices, body(): lax.all_gather(wq_low, 'fsdp', axis=0, tiled=True)  72.7 us
    all_to_all x1, waiting for transfers between devices, body(): lax.all_to_all(wq_first, 'tp', split_axis=1, concat_axis=0, tiled=True)  27.5 us
    all_to_all x1, waiting for transfers between devices, body(): lax.all_to_all(wq_second, 'tp', split_axis=1, concat_axis=0, tiled=True)  26.7 us
    all_to_all x1, waiting for transfers between devices, body(): lax.all_to_all(wq_master, 'tp', split_axis=1, concat_axis=0, tiled=True)  22.8 us
    reduce_sum x1, other arithmetic, body(): jnp.sum(lax.all_gather(kv_term, ('fsdp', 'tp')), axis=0)  21.6 us
    all_to_all x1, waiting for transfers between devices, body(): lax.all_to_all(probe_states, 'fsdp', split_axis=1, concat_axis=0, tiled=T...  13.4 us
  transfers between devices with their start and end apart: 6, of which 6 were waited for; matrix products, arithmetic and copies ran while one was open for 4% of the time, Pallas kernels for 0%

profile of v1, /device:TPU:1, one launch (start us, length us, event | category | flops | bytes accessed | tf_op | source)
XLA Modules:
  0.0 631.3 jit_solution(15751688524574744290)
XLA Ops:
  7.2 3.1 copy.40
  10.3 8.2 %all-to-all-start.1 = ((f32[128,8,512]{2,0,1:T(8,128)}), f32[128,8,512]{2,0,1:T(8,128)S(1)}, u32[]{:S(2)}, u32[]{:S(2)}) async-start(f32[128,8,512]{2,0,1:T(8,128)} %bitcast.41), calls=%async_computation.1 | async-start | bytes 4194304 | tf_op jit(solution)/shard_map/all_to_all | solution.py:35
  18.5 3.1 copy.39
  21.6 27.5 %all-to-all-done.1 = f32[128,8,512]{2,0,1:T(8,128)S(1)} async-done(((f32[128,8,512]{2,0,1:T(8,128)}), f32[128,8,512]{2,0,1:T(8,128)S(1)}, u32[]{:S(2)}, u32[]{:S(2)}) %all-to-all-start.1) | async-done | bytes 2097184 | tf_op jit(solution)/shard_map/all_to_all | solution.py:35
  49.1 1.3 copy-done
  50.4 4.4 all-to-all-start.2
  54.8 3.2 copy.41
  57.9 26.7 %all-to-all-done.2 = f32[128,8,512]{2,0,1:T(8,128)} async-done(((f32[128,8,512]{2,0,1:T(8,128)}), f32[128,8,512]{2,0,1:T(8,128)}, u32[]{:S(2)}, u32[]{:S(2)}) %all-to-all-start.2) | async-done | bytes 2097184 | tf_op jit(solution)/shard_map/all_to_all | solution.py:36
  84.6 3.6 all-to-all-start
  88.2 0.0 all-gather.4.cloned.1.call-start
  88.3 3.3 broadcast_multiply_fusion.1
  91.5 3.3 broadcast_multiply_fusion
  94.8 22.8 %all-to-all-done = f32[128,8,512]{2,0,1:T(8,128)S(1)} async-done(((f32[128,8,512]{2,0,1:T(8,128)}), f32[128,8,512]{2,0,1:T(8,128)S(1)}, u32[]{:S(2)}, u32[]{:S(2)}) %all-to-all-start) | async-done | bytes 2097184 | tf_op jit(solution)/shard_map/all_to_all | solution.py:34
  117.6 6.7 %fusion.7 = (bf16[1024,512]{1,0:T(8,128)(2,1)}, f32[1024,512]{1,0:T(8,128)}, f32[1024,512]{1,0:T(8,128)}, f32[1024,512]{1,0:T(8,128)}) fusion(f32[128,8,512]{2,0,1:T(8,128)S(1)} %all-to-all-done, f32[1024,512]{1,0:T(8,128)} %param.13, f32[128,8,512]{2,0,1:T(8,128)} %broadcast_multiply_fusion, f32[128,8,512]{2,0,1:T(8,128)} %broadcast_multiply_fusion.1), kind=kLoop, calls=%fused_computation.20 | loop fusion | flops 5242880 | bytes 15728640 | tf_op jit(solution)/shard_map/convert_element_type | solution.py:46
  124.3 0.0 copy-start.6
  124.3 0.0 all-gather.4.cloned.1.call-update
  124.4 0.0 copy-done.1
  124.4 0.8 copy.42
  125.2 7.0 %all-to-all-start.3 = ((bf16[16,16,1024]{2,0,1:T(8,128)(2,1)}), bf16[16,16,1024]{2,0,1:T(8,128)(2,1)S(1)}, u32[]{:S(2)}, u32[]{:S(2)}) async-start(bf16[16,16,1024]{2,0,1:T(8,128)(2,1)} %bitcast.38), calls=%async_computation.3 | async-start | bytes 1048576 | tf_op jit(solution)/shard_map/all_to_all | solution.py:40
  132.1 0.0 all-gather.6.cloned.1.call-start
  132.2 0.0 copy-done.3
  132.2 0.0 copy-done.4
  132.2 0.0 copy-done.5
  132.2 0.9 multiply_subtract_fusion
  133.2 13.4 %all-to-all-done.3 = bf16[16,16,1024]{2,0,1:T(8,128)(2,1)S(1)} async-done(((bf16[16,16,1024]{2,0,1:T(8,128)(2,1)}), bf16[16,16,1024]{2,0,1:T(8,128)(2,1)S(1)}, u32[]{:S(2)}, u32[]{:S(2)}) %all-to-all-start.3) | async-done | bytes 524320 | tf_op jit(solution)/shard_map/all_to_all | solution.py:40
  146.6 1.0 fusion.3
  147.6 0.0 all-gather.6.cloned.1.call-update
  147.7 72.7 %all-gather.4.cloned.1.call-done = bf16[16384,512]{1,0:T(8,128)(2,1)} async-done(((bf16[1024,512]{1,0:T(8,128)(2,1)}), bf16[16384,512]{1,0:T(8,128)(2,1)}) %all-gather.4.cloned.1.call-update) | async-done | bytes 16777232 | tf_op jit(solution)/shard_map/all_gather | solution.py:49
  220.4 8.6 %fusion.1 = bf16[16,512]{1,0:T(8,128)(2,1)} fusion(bf16[16,16384]{1,0:T(8,128)(2,1)S(1)} %copy-done.1, bf16[16384,512]{1,0:T(8,128)(2,1)} %all-gather.4.cloned.1.call-done), kind=kOutput, calls=%fused_computation.8 | convolution fusion | flops 268443648 | bytes 17317888 | tf_op jit(solution)/shard_map/dot_general | solution.py:47
  229.0 0.0 copy-done.2
  229.0 373.8 %all-gather.6.cloned.1.call-done = f32[32768,512]{1,0:T(8,128)} async-done(((f32[256,512]{1,0:T(8,128)}), f32[32768,512]{1,0:T(8,128)}) %all-gather.6.cloned.1.call-update) | async-done | bytes 67108880 | tf_op jit(solution)/shard_map/all_gather | solution.py:45
  602.8 21.6 %reduce_sum.9 = bf16[256,512]{1,0:T(8,128)(2,1)} reduce(f32[128,256,512]{2,1,0:T(8,128)} %bitcast.9, f32[]{:T(128)} %constant.2.clone.1), dimensions={0}, to_apply=%region_0.0 | reduce | flops 16646144 | bytes 67371008 | tf_op jit(solution)/shard_map/reduce_sum | solution.py:45
  (7 shorter events, 0.0 us)
Async XLA Ops:
  10.3 38.8 %all-to-all-start.1 = ((f32[128,8,512]{2,0,1:T(8,128)}), f32[128,8,512]{2,0,1:T(8,128)S(1)}, u32[]{:S(2)}, u32[]{:S(2)}) async-start(f32[128,8,512]{2,0,1:T(8,128)} %bitcast.41), calls=%async_computation.1 | async-start | bytes 4194304 | tf_op jit(solution)/shard_map/all_to_all | solution.py:35
  49.1 1.3 copy-start
  50.4 34.2 %all-to-all-start.2 = ((f32[128,8,512]{2,0,1:T(8,128)}), f32[128,8,512]{2,0,1:T(8,128)}, u32[]{:S(2)}, u32[]{:S(2)}) async-start(f32[128,8,512]{2,0,1:T(8,128)} %bitcast.40), calls=%async_computation.2 | async-start | bytes 4194304 | tf_op jit(solution)/shard_map/all_to_all | solution.py:36
  84.6 33.0 %all-to-all-start = ((f32[128,8,512]{2,0,1:T(8,128)}), f32[128,8,512]{2,0,1:T(8,128)S(1)}, u32[]{:S(2)}, u32[]{:S(2)}) async-start(f32[128,8,512]{2,0,1:T(8,128)} %bitcast.39), calls=%async_computation | async-start | bytes 4194304 | tf_op jit(solution)/shard_map/all_to_all | solution.py:34
  88.2 132.2 %all-gather.4.cloned.1.call-start = ((), (), s32[]{:S(2)}) async-start(), calls=%async_computation.4 | async-start | bytes 17825792 | tf_op jit(solution)/shard_map/all_gather | solution.py:49
  94.8 29.6 %copy-start.1 = (bf16[16,16384]{1,0:T(8,128)(2,1)S(1)}, bf16[16,16384]{1,0:T(8,128)(2,1)}, u32[]{:S(2)}) copy-start(bf16[16,16384]{1,0:T(8,128)(2,1)} %param.9) | copy-start | bytes 1572868
  124.3 7.9 %copy-start.3 = (f32[128,512]{1,0:T(8,128)S(1)}, f32[128,512]{1,0:T(8,128)}, u32[]{:S(2)}) copy-start(f32[128,512]{1,0:T(8,128)} %param.14) | copy-start | bytes 786436
  124.3 7.9 %copy-start.4 = (f32[128,512]{1,0:T(8,128)S(1)}, f32[128,512]{1,0:T(8,128)}, u32[]{:S(2)}) copy-start(f32[128,512]{1,0:T(8,128)} %param.17) | copy-start | bytes 786436
  124.3 7.9 %copy-start.5 = (f32[128,512]{1,0:T(8,128)S(1)}, f32[128,512]{1,0:T(8,128)}, u32[]{:S(2)}) copy-start(f32[128,512]{1,0:T(8,128)} %param.16) | copy-start | bytes 786436
  124.3 7.9 %copy-start.6 = (f32[128,512]{1,0:T(8,128)S(1)}, f32[128,512]{1,0:T(8,128)}, u32[]{:S(2)}) copy-start(f32[128,512]{1,0:T(8,128)} %param.15) | copy-start | bytes 786436
  125.2 21.4 %all-to-all-start.3 = ((bf16[16,16,1024]{2,0,1:T(8,128)(2,1)}), bf16[16,16,1024]{2,0,1:T(8,128)(2,1)S(1)}, u32[]{:S(2)}, u32[]{:S(2)}) async-start(bf16[16,16,1024]{2,0,1:T(8,128)(2,1)} %bitcast.38), calls=%async_computation.3 | async-start | bytes 1048576 | tf_op jit(solution)/shard_map/all_to_all | solution.py:40
  132.1 470.7 %all-gather.6.cloned.1.call-start = ((), (), s32[]{:S(2)}) async-start(), calls=%async_computation.5 | async-start | bytes 67633152 | tf_op jit(solution)/shard_map/all_gather | solution.py:45
  133.2 95.8 %copy-start.2 = (f32[128,512]{1,0:T(8,128)}, f32[128,512]{1,0:T(8,128)S(1)}, u32[]{:S(2)}) copy-start(f32[128,512]{1,0:T(8,128)S(1)} %get-tuple-element.12) | copy-start | bytes 786436
Sparse Core Ops, SparseCore 0:
  124.5 95.8 all-gather.3
  222.1 380.7 all-gather.5
